TPU v7x, 512 devices: a whole 4x4x16 slice. The times are simulated.
512 devices in a mesh: blk: 64 (over x, z), grp: 8 (over y, core).
Axes of the slice: x: 4, y: 4, z: 16, core: 2. Of those that a mesh axis runs over, the one named last changes fastest.
Arguments:
- points: bfloat16 [8, 65536, 128], P('grp', 'blk'), may hold values from -4 to 4
- start_panel: bfloat16 [8, 64, 65536], P('grp', None, 'blk'), may hold values from -6 to 6
- seventh: int32 [8, 65536], P('grp', 'blk'), may hold values from 0 to 255, as said below
- neighbours: int32 [8, 256, 16], P('grp'), may hold values from 0 to 255, as said below
- counts: int32 [8, 256], P('grp'), may hold values from 1 to 16, as said below
Outputs:
- ortho_basis: float32 [8, 64, 65536], P('grp', None, 'blk')
- r_factor: float32 [64, 64], replicated
Inputs may be any that keep to these rules, and one draw needn't show every extreme that they name: `seventh`: A point's position within its own block, never the point's own position. `neighbours`: block numbers within the group; block B's owner is B // 4. The listed entries of a block are distinct, never the block itself, and each is owned by an owner whose number differs from B's owner by at most 4 modulo 64. The entries after the listed ones are block numbers of the group and are not used. Of the blocks of one owner, at most 2 are listed by the blocks of another owner together, and exactly 2 for some pairs of owners. `counts`: some block of every group lists 16 blocks.
All inputs are finite; a program needn't handle non-finite values.
Results may differ from a plain program's by a relative error of at most 0.0082.
Values may be sent and summed in bfloat16 or wider, within the bound.
A program may use at most 64 MiB of HBM per device.

v0:
```python
import math
import jax
import jax.numpy as jnp
from jax import lax
from jax.sharding import PartitionSpec as P

E = 128
K = 64
BS = 256
SLOTS = 16
REACH = 4


def passed_along(block, axis, distance):
    devices = range(lax.axis_size(axis))
    route = [((i - distance) % len(devices), i) for i in devices]
    return lax.ppermute(block, axis, route)


def fetch_whole(send_points, send_panel, send_scales, offset):
    return passed_along((send_points, send_panel, send_scales), "blk", offset)


def tile_terms(
    row_points, row_scales, row_norms, col_points, col_panel, col_scales, col_norms, pair_mask
):
    inner_prod = jnp.einsum(
        "pe,cqe->cpq", row_points, col_points, preferred_element_type=jnp.float32
    )
    distance = row_norms[None, :, None] + col_norms[:, None, :] - 2.0 * inner_prod
    denom_scale = (
        row_scales.astype(jnp.float32)[None, :, None] * col_scales.astype(jnp.float32)[:, None, :]
    )
    affinity = jnp.exp(-distance / denom_scale) * pair_mask[:, None, None]
    weights = affinity.astype(jnp.bfloat16)
    carried = jnp.einsum("cpq,kcq->kp", weights, col_panel, preferred_element_type=jnp.float32)
    return (carried, jnp.sum(affinity, axis=(0, 2)))


def local(points, start_panel, seventh, neighbours, counts):
    cycle_size = lax.axis_size("blk")
    my_index = lax.axis_index("blk")
    per_dev = points.shape[1] // BS
    own_points = points[0].reshape(per_dev, BS, E)
    partner_pos = seventh[0].reshape(per_dev, BS)
    partner = jnp.take_along_axis(own_points, partner_pos[:, :, None], axis=1)
    difference = own_points.astype(jnp.float32) - partner.astype(jnp.float32)
    scales = jnp.sqrt(jnp.sum(difference * difference, axis=-1) + 1e-06).astype(jnp.bfloat16)
    as_float = own_points.astype(jnp.float32)
    sq_norm = jnp.sum(as_float * as_float, axis=-1)
    own_panel = start_panel[0].reshape(K, per_dev, BS)
    block_lists = neighbours[0]
    live_mask = jnp.arange(SLOTS, dtype=jnp.int32)[None, :] < counts[0][:, None]
    my_lists = lax.dynamic_slice_in_dim(block_lists, my_index * per_dev, per_dev, 0)
    my_live = lax.dynamic_slice_in_dim(live_mask, my_index * per_dev, per_dev, 0)

    def accumulate(totals, col_points, col_panel, col_scales, col_ids):
        pair_mask = jnp.any(
            (my_lists[:, :, None] == col_ids[None, None, :]) & my_live[:, :, None], axis=1
        ).astype(jnp.float32)
        col_float = col_points.astype(jnp.float32)
        col_norms = jnp.sum(col_float * col_float, axis=-1)

        def per_block(inputs):
            row_points, row_scales, row_norms, row_mask = inputs
            return tile_terms(
                row_points,
                row_scales,
                row_norms,
                col_points,
                col_panel,
                col_scales,
                col_norms,
                row_mask,
            )

        carried, degree = lax.map(per_block, (own_points, scales, sq_norm, pair_mask))
        return (totals[0] + carried, totals[1] + degree)

    totals = (jnp.zeros((per_dev, K, BS), jnp.float32), jnp.zeros((per_dev, BS), jnp.float32))
    local_ids = my_index * per_dev + jnp.arange(per_dev, dtype=jnp.int32)
    totals = accumulate(totals, own_points, own_panel, scales, local_ids)
    for offset in list(range(1, REACH + 1)) + list(range(-REACH, 0)):
        source = (my_index - offset) % cycle_size
        col_points, col_panel, col_scales = fetch_whole(own_points, own_panel, scales, offset)
        col_ids = source * per_dev + jnp.arange(per_dev, dtype=jnp.int32)
        totals = accumulate(totals, col_points, col_panel, col_scales, col_ids)
    carried = jnp.transpose(totals[0], (1, 0, 2))
    degree = 1.0 + totals[1]
    walked = ((own_panel.astype(jnp.float32) + carried) / degree[None, :, :]).reshape(
        K, per_dev * BS
    )
    gram_local = jnp.dot(
        walked, walked.T, precision=lax.Precision.HIGHEST, preferred_element_type=jnp.float32
    )
    gram_matrix = lax.psum(gram_local, ("blk", "grp"))
    lower_factor = jnp.linalg.cholesky(gram_matrix)
    solved = lax.linalg.triangular_solve(lower_factor, walked, left_side=True, lower=True)
    point_total = points.shape[1] * lax.axis_size("blk") * lax.axis_size("grp")
    root_count = math.sqrt(point_total)
    ortho_basis = (solved * root_count)[None]
    r_factor = lower_factor.T / root_count
    return (ortho_basis, r_factor)


def solution(mesh):
    in_specs = (
        P("grp", "blk", None),
        P("grp", None, "blk"),
        P("grp", "blk"),
        P("grp", None, None),
        P("grp", None),
    )
    out_specs = (P("grp", None, "blk"), P())
    return jax.shard_map(local, mesh=mesh, in_specs=in_specs, out_specs=out_specs, check_vma=False)
```

profile of v0, /device:TPU:1, one launch (start us, length us, event | category | flops | bytes accessed | tf_op | source)
XLA Modules:
  0.0 331.3 jit_solution(13664249299728064872)
XLA Ops:
  1.6 4.4 %collective-permute-start.2 = (bf16[64,4,256]{2,1,0:T(4,128)(2,1)S(1)}, bf16[64,4,256]{2,1,0:T(4,128)(2,1)S(1)}, u32[]{:S(2)}, u32[]{:S(2)}) collective-permute-start(bf16[64,4,256]{2,1,0:T(4,128)(2,1)S(1)} %reshape_squeeze.6), channel_id=1, source_target_pairs={{504,0},{0,8},{8,16},{16,24},{24,32},{32,40},{40,48},{48,56},{56,6... | collective-permute-start | bytes 393224 | tf_op jit(solution)/shard_map/ppermute | solution.py:17
  6.0 4.9 %collective-permute-start.5 = (bf16[64,4,256]{2,1,0:T(4,128)(2,1)S(1)}, bf16[64,4,256]{2,1,0:T(4,128)(2,1)S(1)}, u32[]{:S(2)}, u32[]{:S(2)}) collective-permute-start(bf16[64,4,256]{2,1,0:T(4,128)(2,1)S(1)} %reshape_squeeze.6), channel_id=1, source_target_pairs={{496,0},{504,8},{0,16},{8,24},{16,32},{24,40},{32,48},{40,56},{48,... | collective-permute-start | bytes 393224 | tf_op jit(solution)/shard_map/ppermute | solution.py:17
  10.9 7.5 %collective-permute-start.8 = (bf16[64,4,256]{2,1,0:T(4,128)(2,1)S(1)}, bf16[64,4,256]{2,1,0:T(4,128)(2,1)S(1)}, u32[]{:S(2)}, u32[]{:S(2)}) collective-permute-start(bf16[64,4,256]{2,1,0:T(4,128)(2,1)S(1)} %reshape_squeeze.6), channel_id=1, source_target_pairs={{488,0},{496,8},{504,16},{0,24},{8,32},{16,40},{24,48},{32,56},{40... | collective-permute-start | bytes 393224 | tf_op jit(solution)/shard_map/ppermute | solution.py:17
  18.4 7.0 %collective-permute-start.11 = (bf16[64,4,256]{2,1,0:T(4,128)(2,1)S(1)}, bf16[64,4,256]{2,1,0:T(4,128)(2,1)S(1)}, u32[]{:S(2)}, u32[]{:S(2)}) collective-permute-start(bf16[64,4,256]{2,1,0:T(4,128)(2,1)S(1)} %reshape_squeeze.6), channel_id=1, source_target_pairs={{480,0},{488,8},{496,16},{504,24},{0,32},{8,40},{16,48},{24,56},{3... | collective-permute-start | bytes 393224 | tf_op jit(solution)/shard_map/ppermute | solution.py:17
  25.4 2.6 collective-permute-start
  30.2 6.8 %gather_fusion = bf16[1024,128]{1,0:T(8,128)(2,1)S(1)} fusion(bf16[4,256,128]{2,1,0:T(8,128)(2,1)} %bitcast.90, s32[1024]{0:T(1024)S(1)} %bitcast.504), kind=kCustom, calls=%fused_computation | custom fusion | bytes 532480 | tf_op jit(solution)/shard_map/jit(take_along_axis)/gather | solution.py:46
  40.1 5.2 %collective-permute-start.14 = (bf16[64,4,256]{2,1,0:T(4,128)(2,1)S(1)}, bf16[64,4,256]{2,1,0:T(4,128)(2,1)S(1)}, u32[]{:S(2)}, u32[]{:S(2)}) collective-permute-start(bf16[64,4,256]{2,1,0:T(4,128)(2,1)S(1)} %reshape_squeeze.6), channel_id=1, source_target_pairs={{32,0},{40,8},{48,16},{56,24},{64,32},{72,40},{80,48},{88,56},{96,... | collective-permute-start | bytes 393224 | tf_op jit(solution)/shard_map/ppermute | solution.py:17
  45.3 3.6 %collective-permute-start.17 = (bf16[64,4,256]{2,1,0:T(4,128)(2,1)S(1)}, bf16[64,4,256]{2,1,0:T(4,128)(2,1)S(1)}, u32[]{:S(2)}, u32[]{:S(2)}) collective-permute-start(bf16[64,4,256]{2,1,0:T(4,128)(2,1)S(1)} %reshape_squeeze.6), channel_id=1, source_target_pairs={{24,0},{32,8},{40,16},{48,24},{56,32},{64,40},{72,48},{80,56},{88,... | collective-permute-start | bytes 393224 | tf_op jit(solution)/shard_map/ppermute | solution.py:17
  48.9 3.7 %collective-permute-start.20 = (bf16[64,4,256]{2,1,0:T(4,128)(2,1)S(1)}, bf16[64,4,256]{2,1,0:T(4,128)(2,1)S(1)}, u32[]{:S(2)}, u32[]{:S(2)}) collective-permute-start(bf16[64,4,256]{2,1,0:T(4,128)(2,1)S(1)} %reshape_squeeze.6), channel_id=1, source_target_pairs={{16,0},{24,8},{32,16},{40,24},{48,32},{56,40},{64,48},{72,56},{80,... | collective-permute-start | bytes 393224 | tf_op jit(solution)/shard_map/ppermute | solution.py:17
  52.5 3.1 collective-permute-start.23
  55.7 13.1 %while.109 = (s32[]{:T(128)}, f32[4,64,256]{2,1,0:T(8,128)S(1)}, f32[4,256]{1,0:T(4,128)S(1)}, f32[4,256]{1,0:T(4,128)S(1)}, bf16[4,256,128]{2,1,0:T(8,128)(2,1)...) while((s32[]{:T(128)}, f32[4,64,256]{2,1,0:T(8,128)S(1)}, ...), condition=%wide.region_5.6_spmd, body=%wide.region_3.0_spmd.sunk | while | flops 103023616 | bytes 1596585 | solution.py:77
  71.2 2.5 collective-permute-start.4
  73.7 5.2 %collective-permute-start.3 = (bf16[4,256,128]{2,1,0:T(8,128)(2,1)}, bf16[4,256,128]{2,1,0:T(8,128)(2,1)S(1)}, u32[]{:S(2)}, u32[]{:S(2)}) collective-permute-start(bf16[4,256,128]{2,1,0:T(8,128)(2,1)} %bitcast.90), channel_id=1, source_target_pairs={{496,0},{504,8},{0,16},{8,24},{16,32},{24,40},{32,48},{40,56},{48,... | collective-permute-start | bytes 786440 | tf_op jit(solution)/shard_map/ppermute | solution.py:17
  79.0 5.9 %collective-permute-start.7 = (bf16[4,256]{1,0:T(4,128)(2,1)}, bf16[4,256]{1,0:T(4,128)(2,1)S(1)}, u32[]{:S(2)}, u32[]{:S(2)}) collective-permute-start(bf16[4,256]{1,0:T(4,128)(2,1)} %convert_element_type.264), channel_id=1, source_target_pairs={{488,0},{496,8},{504,16},{0,24},{8,32},{16,40},{24,48},{32,56},{40... | collective-permute-start | bytes 6152 | tf_op jit(solution)/shard_map/ppermute | solution.py:17
  85.0 2.4 collective-permute-start.6
  89.5 9.6 %while.110 = (s32[]{:T(128)}, f32[4,64,256]{2,1,0:T(8,128)S(1)}, f32[4,256]{1,0:T(4,128)S(1)}, f32[4,256]{1,0:T(4,128)S(1)}, f32[4,256]{1,0:T(4,128)S(1)}, /*ind...) while((s32[]{:T(128)}, f32[4,64,256]{2,1,0:T(8,128)S(1)}, ...), condition=%wide.region_10.11_spmd, body=%wide.region_8.10_spmd.sunk | while | flops 103023616 | bytes 1596609 | solution.py:77
  99.2 4.9 %collective-permute-start.9 = (bf16[4,256,128]{2,1,0:T(8,128)(2,1)}, bf16[4,256,128]{2,1,0:T(8,128)(2,1)S(1)}, u32[]{:S(2)}, u32[]{:S(2)}) collective-permute-start(bf16[4,256,128]{2,1,0:T(8,128)(2,1)} %bitcast.90), channel_id=1, source_target_pairs={{480,0},{488,8},{496,16},{504,24},{0,32},{8,40},{16,48},{24,56},{3... | collective-permute-start | bytes 786440 | tf_op jit(solution)/shard_map/ppermute | solution.py:17
  104.3 6.4 %collective-permute-start.13 = (bf16[4,256]{1,0:T(4,128)(2,1)}, bf16[4,256]{1,0:T(4,128)(2,1)S(1)}, u32[]{:S(2)}, u32[]{:S(2)}) collective-permute-start(bf16[4,256]{1,0:T(4,128)(2,1)} %convert_element_type.264), channel_id=1, source_target_pairs={{32,0},{40,8},{48,16},{56,24},{64,32},{72,40},{80,48},{88,56},{96,... | collective-permute-start | bytes 6152 | tf_op jit(solution)/shard_map/ppermute | solution.py:17
  110.8 9.6 %while.111 = (s32[]{:T(128)}, f32[4,64,256]{2,1,0:T(8,128)S(1)}, f32[4,256]{1,0:T(4,128)S(1)}, f32[4,256]{1,0:T(4,128)S(1)}, f32[4,256]{1,0:T(4,128)S(1)}, /*ind...) while((s32[]{:T(128)}, f32[4,64,256]{2,1,0:T(8,128)S(1)}, ...), condition=%wide.region_15.16_spmd, body=%wide.region_13.15_spmd.sunk | while | flops 103023616 | bytes 1596609 | solution.py:77
  120.4 7.3 %collective-permute-start.12 = (bf16[4,256,128]{2,1,0:T(8,128)(2,1)}, bf16[4,256,128]{2,1,0:T(8,128)(2,1)S(1)}, u32[]{:S(2)}, u32[]{:S(2)}) collective-permute-start(bf16[4,256,128]{2,1,0:T(8,128)(2,1)} %bitcast.90), channel_id=1, source_target_pairs={{32,0},{40,8},{48,16},{56,24},{64,32},{72,40},{80,48},{88,56},{96,... | collective-permute-start | bytes 786440 | tf_op jit(solution)/shard_map/ppermute | solution.py:17
  127.9 5.9 %collective-permute-start.16 = (bf16[4,256]{1,0:T(4,128)(2,1)}, bf16[4,256]{1,0:T(4,128)(2,1)S(1)}, u32[]{:S(2)}, u32[]{:S(2)}) collective-permute-start(bf16[4,256]{1,0:T(4,128)(2,1)} %convert_element_type.264), channel_id=1, source_target_pairs={{24,0},{32,8},{40,16},{48,24},{56,32},{64,40},{72,48},{80,56},{88,... | collective-permute-start | bytes 6152 | tf_op jit(solution)/shard_map/ppermute | solution.py:17
  133.9 9.6 %while.112 = (s32[]{:T(128)}, f32[4,64,256]{2,1,0:T(8,128)S(1)}, f32[4,256]{1,0:T(4,128)S(1)}, f32[4,256]{1,0:T(4,128)S(1)}, f32[4,256]{1,0:T(4,128)S(1)}, /*ind...) while((s32[]{:T(128)}, f32[4,64,256]{2,1,0:T(8,128)S(1)}, ...), condition=%wide.region_20.21_spmd, body=%wide.region_18.20_spmd.sunk | while | flops 103023616 | bytes 1596609 | solution.py:77
  148.1 9.6 %while.113 = (s32[]{:T(128)}, f32[4,64,256]{2,1,0:T(8,128)S(1)}, f32[4,256]{1,0:T(4,128)S(1)}, f32[4,256]{1,0:T(4,128)S(1)}, f32[4,256]{1,0:T(4,128)S(1)}, /*ind...) while((s32[]{:T(128)}, f32[4,64,256]{2,1,0:T(8,128)S(1)}, ...), condition=%wide.region_25.26_spmd, body=%wide.region_23.25_spmd.sunk | while | flops 103023616 | bytes 1596609 | solution.py:77
  157.7 4.8 %collective-permute-start.18 = (bf16[4,256,128]{2,1,0:T(8,128)(2,1)}, bf16[4,256,128]{2,1,0:T(8,128)(2,1)S(1)}, u32[]{:S(2)}, u32[]{:S(2)}) collective-permute-start(bf16[4,256,128]{2,1,0:T(8,128)(2,1)} %bitcast.90), channel_id=1, source_target_pairs={{16,0},{24,8},{32,16},{40,24},{48,32},{56,40},{64,48},{72,56},{80,... | collective-permute-start | bytes 786440 | tf_op jit(solution)/shard_map/ppermute | solution.py:17
  162.8 3.1 collective-permute-start.22
  165.9 9.6 %while.114 = (s32[]{:T(128)}, f32[4,64,256]{2,1,0:T(8,128)S(1)}, f32[4,256]{1,0:T(4,128)S(1)}, f32[4,256]{1,0:T(4,128)S(1)}, f32[4,256]{1,0:T(4,128)S(1)}, /*ind...) while((s32[]{:T(128)}, f32[4,64,256]{2,1,0:T(8,128)S(1)}, ...), condition=%wide.region_30.31_spmd, body=%wide.region_28.30_spmd.sunk | while | flops 103023616 | bytes 1596609 | solution.py:77
  177.9 9.6 %while.115 = (s32[]{:T(128)}, f32[4,64,256]{2,1,0:T(8,128)S(1)}, f32[4,256]{1,0:T(4,128)S(1)}, f32[4,256]{1,0:T(4,128)S(1)}, f32[4,256]{1,0:T(4,128)S(1)}, /*ind...) while((s32[]{:T(128)}, f32[4,64,256]{2,1,0:T(8,128)S(1)}, ...), condition=%wide.region_35.36_spmd, body=%wide.region_33.35_spmd.sunk | while | flops 103023616 | bytes 1596609 | solution.py:77
  187.8 9.6 %while.116 = (s32[]{:T(128)}, f32[4,64,256]{2,1,0:T(8,128)S(1)}, f32[4,256]{1,0:T(4,128)S(1)}, f32[4,256]{1,0:T(4,128)S(1)}, f32[4,256]{1,0:T(4,128)S(1)}, /*ind...) while((s32[]{:T(128)}, f32[4,64,256]{2,1,0:T(8,128)S(1)}, ...), condition=%wide.region_40.41_spmd, body=%wide.region_38.40_spmd.sunk | while | flops 103023616 | bytes 1596609 | solution.py:77
  198.7 10.2 %while.117 = (s32[]{:T(128)}, f32[4,64,256]{2,1,0:T(8,128)S(1)}, f32[4,256]{1,0:T(4,128)S(1)}, f32[4,256]{1,0:T(4,128)S(1)}, f32[4,256]{1,0:T(4,128)S(1)}, /*ind...) while((s32[]{:T(128)}, f32[4,64,256]{2,1,0:T(8,128)S(1)}, ...), condition=%wide.region_45.46_spmd, body=%wide.region_43.45_spmd.sunk | while | flops 103023616 | bytes 1596609 | solution.py:77
  209.5 107.8 %psum.7 = f32[64,64]{0,1:T(8,128)S(1)} all-reduce(f32[64,64]{0,1:T(8,128)S(1)} %convolution_bitcast_fusion.9), channel_id=1, replica_groups=mesh['blk'=64,'grp'=8] {'blk','grp'}, use_global_device_ids=true, to_apply=%region_46.47 | all-reduce | flops 4096 | bytes 32768 | tf_op jit(solution)/shard_map/psum | solution.py:96
  317.3 5.8 %cholesky.16 = f32[64,64]{1,0:T(8,128)S(1)} custom-call(f32[64,64]{1,0:T(8,128)S(1)} %fusion.123), custom_call_target="Cholesky" | custom-call | tf_op jit(solution)/shard_map/jit(cholesky)/cholesky | solution.py:97
  324.5 4.9 %custom-call.6 = f32[1,64,64]{1,2,0:T(8,128)S(1)} custom-call(f32[1,64,64]{2,1,0:T(8,128)S(1)} %get-tuple-element.1067), custom_call_target="InvertDiagBlocksLowerTriangular" | custom-call | tf_op jit(solution)/shard_map/triangular_solve | solution.py:98
  (363 shorter events, 112.6 us)
Async XLA Ops:
  0.6 27.6 %copy-start = (s32[1,256,16]{1,2,0:T(8,128)S(1)}, s32[1,256,16]{1,2,0:T(8,128)}, u32[]{:S(2)}) copy-start(s32[1,256,16]{1,2,0:T(8,128)} %param.26) | copy-start | bytes 49156
  1.6 38.4 %collective-permute-start.2 = (bf16[64,4,256]{2,1,0:T(4,128)(2,1)S(1)}, bf16[64,4,256]{2,1,0:T(4,128)(2,1)S(1)}, u32[]{:S(2)}, u32[]{:S(2)}) collective-permute-start(bf16[64,4,256]{2,1,0:T(4,128)(2,1)S(1)} %reshape_squeeze.6), channel_id=1, source_target_pairs={{504,0},{0,8},{8,16},{16,24},{24,32},{32,40},{40,48},{48,56},{56,6... | collective-permute-start | bytes 393224 | tf_op jit(solution)/shard_map/ppermute | solution.py:17
  6.0 39.2 %collective-permute-start.5 = (bf16[64,4,256]{2,1,0:T(4,128)(2,1)S(1)}, bf16[64,4,256]{2,1,0:T(4,128)(2,1)S(1)}, u32[]{:S(2)}, u32[]{:S(2)}) collective-permute-start(bf16[64,4,256]{2,1,0:T(4,128)(2,1)S(1)} %reshape_squeeze.6), channel_id=1, source_target_pairs={{496,0},{504,8},{0,16},{8,24},{16,32},{24,40},{32,48},{40,56},{48,... | collective-permute-start | bytes 393224 | tf_op jit(solution)/shard_map/ppermute | solution.py:17
  10.9 37.9 %collective-permute-start.8 = (bf16[64,4,256]{2,1,0:T(4,128)(2,1)S(1)}, bf16[64,4,256]{2,1,0:T(4,128)(2,1)S(1)}, u32[]{:S(2)}, u32[]{:S(2)}) collective-permute-start(bf16[64,4,256]{2,1,0:T(4,128)(2,1)S(1)} %reshape_squeeze.6), channel_id=1, source_target_pairs={{488,0},{496,8},{504,16},{0,24},{8,32},{16,40},{24,48},{32,56},{40... | collective-permute-start | bytes 393224 | tf_op jit(solution)/shard_map/ppermute | solution.py:17
  18.4 34.1 %collective-permute-start.11 = (bf16[64,4,256]{2,1,0:T(4,128)(2,1)S(1)}, bf16[64,4,256]{2,1,0:T(4,128)(2,1)S(1)}, u32[]{:S(2)}, u32[]{:S(2)}) collective-permute-start(bf16[64,4,256]{2,1,0:T(4,128)(2,1)S(1)} %reshape_squeeze.6), channel_id=1, source_target_pairs={{480,0},{488,8},{496,16},{504,24},{0,32},{8,40},{16,48},{24,56},{3... | collective-permute-start | bytes 393224 | tf_op jit(solution)/shard_map/ppermute | solution.py:17
  25.4 59.5 %collective-permute-start = (bf16[4,256,128]{2,1,0:T(8,128)(2,1)}, bf16[4,256,128]{2,1,0:T(8,128)(2,1)S(1)}, u32[]{:S(2)}, u32[]{:S(2)}) collective-permute-start(bf16[4,256,128]{2,1,0:T(8,128)(2,1)} %bitcast.90), channel_id=1, source_target_pairs={{504,0},{0,8},{8,16},{16,24},{24,32},{32,40},{40,48},{48,56},{56,6... | collective-permute-start | bytes 786440 | tf_op jit(solution)/shard_map/ppermute | solution.py:17
  28.2 0.7 copy-start.2
  28.3 1.3 copy-start.1
  40.1 28.9 %collective-permute-start.14 = (bf16[64,4,256]{2,1,0:T(4,128)(2,1)S(1)}, bf16[64,4,256]{2,1,0:T(4,128)(2,1)S(1)}, u32[]{:S(2)}, u32[]{:S(2)}) collective-permute-start(bf16[64,4,256]{2,1,0:T(4,128)(2,1)S(1)} %reshape_squeeze.6), channel_id=1, source_target_pairs={{32,0},{40,8},{48,16},{56,24},{64,32},{72,40},{80,48},{88,56},{96,... | collective-permute-start | bytes 393224 | tf_op jit(solution)/shard_map/ppermute | solution.py:17
  45.3 25.9 %collective-permute-start.17 = (bf16[64,4,256]{2,1,0:T(4,128)(2,1)S(1)}, bf16[64,4,256]{2,1,0:T(4,128)(2,1)S(1)}, u32[]{:S(2)}, u32[]{:S(2)}) collective-permute-start(bf16[64,4,256]{2,1,0:T(4,128)(2,1)S(1)} %reshape_squeeze.6), channel_id=1, source_target_pairs={{24,0},{32,8},{40,16},{48,24},{56,32},{64,40},{72,48},{80,56},{88,... | collective-permute-start | bytes 393224 | tf_op jit(solution)/shard_map/ppermute | solution.py:17
  48.9 24.9 %collective-permute-start.20 = (bf16[64,4,256]{2,1,0:T(4,128)(2,1)S(1)}, bf16[64,4,256]{2,1,0:T(4,128)(2,1)S(1)}, u32[]{:S(2)}, u32[]{:S(2)}) collective-permute-start(bf16[64,4,256]{2,1,0:T(4,128)(2,1)S(1)} %reshape_squeeze.6), channel_id=1, source_target_pairs={{16,0},{24,8},{32,16},{40,24},{48,32},{56,40},{64,48},{72,56},{80,... | collective-permute-start | bytes 393224 | tf_op jit(solution)/shard_map/ppermute | solution.py:17
  52.5 26.4 %collective-permute-start.23 = (bf16[64,4,256]{2,1,0:T(4,128)(2,1)S(1)}, bf16[64,4,256]{2,1,0:T(4,128)(2,1)S(1)}, u32[]{:S(2)}, u32[]{:S(2)}) collective-permute-start(bf16[64,4,256]{2,1,0:T(4,128)(2,1)S(1)} %reshape_squeeze.6), channel_id=1, source_target_pairs={{8,0},{16,8},{24,16},{32,24},{40,32},{48,40},{56,48},{64,56},{72,6... | collective-permute-start | bytes 393224 | tf_op jit(solution)/shard_map/ppermute | solution.py:17
  68.9 18.6 %collective-permute-start.1 = (bf16[4,256]{1,0:T(4,128)(2,1)}, bf16[4,256]{1,0:T(4,128)(2,1)S(1)}, u32[]{:S(2)}, u32[]{:S(2)}) collective-permute-start(bf16[4,256]{1,0:T(4,128)(2,1)} %convert_element_type.264), channel_id=1, source_target_pairs={{504,0},{0,8},{8,16},{16,24},{24,32},{32,40},{40,48},{48,56},{56,6... | collective-permute-start | bytes 6152 | tf_op jit(solution)/shard_map/ppermute | solution.py:17
  71.2 33.1 %collective-permute-start.4 = (bf16[4,256]{1,0:T(4,128)(2,1)}, bf16[4,256]{1,0:T(4,128)(2,1)S(1)}, u32[]{:S(2)}, u32[]{:S(2)}) collective-permute-start(bf16[4,256]{1,0:T(4,128)(2,1)} %convert_element_type.264), channel_id=1, source_target_pairs={{496,0},{504,8},{0,16},{8,24},{16,32},{24,40},{32,48},{40,56},{48,... | collective-permute-start | bytes 6152 | tf_op jit(solution)/shard_map/ppermute | solution.py:17
  73.7 25.4 %collective-permute-start.3 = (bf16[4,256,128]{2,1,0:T(8,128)(2,1)}, bf16[4,256,128]{2,1,0:T(8,128)(2,1)S(1)}, u32[]{:S(2)}, u32[]{:S(2)}) collective-permute-start(bf16[4,256,128]{2,1,0:T(8,128)(2,1)} %bitcast.90), channel_id=1, source_target_pairs={{496,0},{504,8},{0,16},{8,24},{16,32},{24,40},{32,48},{40,56},{48,... | collective-permute-start | bytes 786440 | tf_op jit(solution)/shard_map/ppermute | solution.py:17
  79.0 48.9 %collective-permute-start.7 = (bf16[4,256]{1,0:T(4,128)(2,1)}, bf16[4,256]{1,0:T(4,128)(2,1)S(1)}, u32[]{:S(2)}, u32[]{:S(2)}) collective-permute-start(bf16[4,256]{1,0:T(4,128)(2,1)} %convert_element_type.264), channel_id=1, source_target_pairs={{488,0},{496,8},{504,16},{0,24},{8,32},{16,40},{24,48},{32,56},{40... | collective-permute-start | bytes 6152 | tf_op jit(solution)/shard_map/ppermute | solution.py:17
  85.0 35.4 %collective-permute-start.6 = (bf16[4,256,128]{2,1,0:T(8,128)(2,1)}, bf16[4,256,128]{2,1,0:T(8,128)(2,1)S(1)}, u32[]{:S(2)}, u32[]{:S(2)}) collective-permute-start(bf16[4,256,128]{2,1,0:T(8,128)(2,1)} %bitcast.90), channel_id=1, source_target_pairs={{488,0},{496,8},{504,16},{0,24},{8,32},{16,40},{24,48},{32,56},{40... | collective-permute-start | bytes 786440 | tf_op jit(solution)/shard_map/ppermute | solution.py:17
  87.6 58.5 %collective-permute-start.10 = (bf16[4,256]{1,0:T(4,128)(2,1)}, bf16[4,256]{1,0:T(4,128)(2,1)S(1)}, u32[]{:S(2)}, u32[]{:S(2)}) collective-permute-start(bf16[4,256]{1,0:T(4,128)(2,1)} %convert_element_type.264), channel_id=1, source_target_pairs={{480,0},{488,8},{496,16},{504,24},{0,32},{8,40},{16,48},{24,56},{3... | collective-permute-start | bytes 6152 | tf_op jit(solution)/shard_map/ppermute | solution.py:17
  99.2 44.3 %collective-permute-start.9 = (bf16[4,256,128]{2,1,0:T(8,128)(2,1)}, bf16[4,256,128]{2,1,0:T(8,128)(2,1)S(1)}, u32[]{:S(2)}, u32[]{:S(2)}) collective-permute-start(bf16[4,256,128]{2,1,0:T(8,128)(2,1)} %bitcast.90), channel_id=1, source_target_pairs={{480,0},{488,8},{496,16},{504,24},{0,32},{8,40},{16,48},{24,56},{3... | collective-permute-start | bytes 786440 | tf_op jit(solution)/shard_map/ppermute | solution.py:17
  104.3 58.5 %collective-permute-start.13 = (bf16[4,256]{1,0:T(4,128)(2,1)}, bf16[4,256]{1,0:T(4,128)(2,1)S(1)}, u32[]{:S(2)}, u32[]{:S(2)}) collective-permute-start(bf16[4,256]{1,0:T(4,128)(2,1)} %convert_element_type.264), channel_id=1, source_target_pairs={{32,0},{40,8},{48,16},{56,24},{64,32},{72,40},{80,48},{88,56},{96,... | collective-permute-start | bytes 6152 | tf_op jit(solution)/shard_map/ppermute | solution.py:17
  120.4 37.3 %collective-permute-start.12 = (bf16[4,256,128]{2,1,0:T(8,128)(2,1)}, bf16[4,256,128]{2,1,0:T(8,128)(2,1)S(1)}, u32[]{:S(2)}, u32[]{:S(2)}) collective-permute-start(bf16[4,256,128]{2,1,0:T(8,128)(2,1)} %bitcast.90), channel_id=1, source_target_pairs={{32,0},{40,8},{48,16},{56,24},{64,32},{72,40},{80,48},{88,56},{96,... | collective-permute-start | bytes 786440 | tf_op jit(solution)/shard_map/ppermute | solution.py:17
  127.9 49.9 %collective-permute-start.16 = (bf16[4,256]{1,0:T(4,128)(2,1)}, bf16[4,256]{1,0:T(4,128)(2,1)S(1)}, u32[]{:S(2)}, u32[]{:S(2)}) collective-permute-start(bf16[4,256]{1,0:T(4,128)(2,1)} %convert_element_type.264), channel_id=1, source_target_pairs={{24,0},{32,8},{40,16},{48,24},{56,32},{64,40},{72,48},{80,56},{88,... | collective-permute-start | bytes 6152 | tf_op jit(solution)/shard_map/ppermute | solution.py:17
  143.5 32.0 %collective-permute-start.15 = (bf16[4,256,128]{2,1,0:T(8,128)(2,1)}, bf16[4,256,128]{2,1,0:T(8,128)(2,1)S(1)}, u32[]{:S(2)}, u32[]{:S(2)}) collective-permute-start(bf16[4,256,128]{2,1,0:T(8,128)(2,1)} %bitcast.90), channel_id=1, source_target_pairs={{24,0},{32,8},{40,16},{48,24},{56,32},{64,40},{72,48},{80,56},{88,... | collective-permute-start | bytes 786440 | tf_op jit(solution)/shard_map/ppermute | solution.py:17
  146.1 41.7 %collective-permute-start.19 = (bf16[4,256]{1,0:T(4,128)(2,1)}, bf16[4,256]{1,0:T(4,128)(2,1)S(1)}, u32[]{:S(2)}, u32[]{:S(2)}) collective-permute-start(bf16[4,256]{1,0:T(4,128)(2,1)} %convert_element_type.264), channel_id=1, source_target_pairs={{16,0},{24,8},{32,16},{40,24},{48,32},{56,40},{64,48},{72,56},{80,... | collective-permute-start | bytes 6152 | tf_op jit(solution)/shard_map/ppermute | solution.py:17
  157.7 29.8 %collective-permute-start.18 = (bf16[4,256,128]{2,1,0:T(8,128)(2,1)}, bf16[4,256,128]{2,1,0:T(8,128)(2,1)S(1)}, u32[]{:S(2)}, u32[]{:S(2)}) collective-permute-start(bf16[4,256,128]{2,1,0:T(8,128)(2,1)} %bitcast.90), channel_id=1, source_target_pairs={{16,0},{24,8},{32,16},{40,24},{48,32},{56,40},{64,48},{72,56},{80,... | collective-permute-start | bytes 786440 | tf_op jit(solution)/shard_map/ppermute | solution.py:17
  162.8 35.9 %collective-permute-start.22 = (bf16[4,256]{1,0:T(4,128)(2,1)}, bf16[4,256]{1,0:T(4,128)(2,1)S(1)}, u32[]{:S(2)}, u32[]{:S(2)}) collective-permute-start(bf16[4,256]{1,0:T(4,128)(2,1)} %convert_element_type.264), channel_id=1, source_target_pairs={{8,0},{16,8},{24,16},{32,24},{40,32},{48,40},{56,48},{64,56},{72,6... | collective-permute-start | bytes 6152 | tf_op jit(solution)/shard_map/ppermute | solution.py:17
  175.5 21.9 %collective-permute-start.21 = (bf16[4,256,128]{2,1,0:T(8,128)(2,1)}, bf16[4,256,128]{2,1,0:T(8,128)(2,1)}, u32[]{:S(2)}, u32[]{:S(2)}) collective-permute-start(bf16[4,256,128]{2,1,0:T(8,128)(2,1)} %bitcast.90), channel_id=1, source_target_pairs={{8,0},{16,8},{24,16},{32,24},{40,32},{48,40},{56,48},{64,56},{72,6... | collective-permute-start | bytes 786440 | tf_op jit(solution)/shard_map/ppermute | solution.py:17
where the time goes:
time: 335 us; the launch traced here: 331 us
  blocking collectives  108 us (32%)
  starting transfers between devices  101 us (30%)
  matrix products  60.8 us (18%)
  other arithmetic  45.7 us (14%)
  local copies, waits for them, and re-layouts  12.9 us (4%)
    psum x1, blocking collectives, local(): gram_matrix = lax.psum(gram_local, ('blk', 'grp'))  108 us
    ppermute x24, starting transfers between devices, passed_along(): return lax.ppermute(block, axis, route)  101 us
    dot_general x36, matrix products, tile_terms(): jnp.einsum('pe,cqe->cpq', row_points, col_points, preferred_element_type=...  51.8 us
    convert_element_type x36, other arithmetic, tile_terms(): row_scales.astype(jnp.float32)[None, :, None]  24.9 us
    dot_general x36, matrix products, tile_terms(): jnp.einsum('cpq,kcq->kp', weights, col_panel, preferred_element_type=jnp....  7.53 us
    gather x1, local copies, waits for them, and re-layouts, local(): partner = jnp.take_along_axis(own_points, partner_pos[:, :, None], axis=1)  6.76 us
  transfers between devices with their start and end apart: 24, of which 0 were waited for; matrix products, arithmetic and copies ran while one was open for 28% of the time, Pallas kernels for 0%

commit v1 on v0

--- a/solution.py
+++ b/solution.py
@@ -93,7 +93,7 @@
     gram_local = jnp.dot(
         walked, walked.T, precision=lax.Precision.HIGHEST, preferred_element_type=jnp.float32
     )
-    gram_matrix = lax.psum(gram_local, ("blk", "grp"))
+    gram_matrix = jnp.sum(lax.all_gather(gram_local, ("blk", "grp")), axis=0)
     lower_factor = jnp.linalg.cholesky(gram_matrix)
     solved = lax.linalg.triangular_solve(lower_factor, walked, left_side=True, lower=True)
     point_total = points.shape[1] * lax.axis_size("blk") * lax.axis_size("grp")

time: 335 us -> 472 us (1.41)
  waiting for transfers between devices: 0.06 us -> 222 us
  blocking collectives: 108 us -> 0 us
  between operations: 1.63 us -> 15 us
  other arithmetic: 45.7 us -> 54.1 us
    all_gather x0 -> x1, waiting for transfers between devices: none -> 222 us  [local(): gram_matrix = jnp.sum(lax.all_gather(gram_local, ('blk', 'grp')), axis=0)]
    psum x1 -> x0, blocking collectives: 108 us -> none  [local(): gram_matrix = lax.psum(gram_local, ('blk', 'grp'))]
    reduce_sum x0 -> x1, other arithmetic: none -> 6.94 us  [local(): gram_matrix = jnp.sum(lax.all_gather(gram_local, ('blk', 'grp')), axis=0)]
  transfers between devices with their start and end apart: 24 -> 25, of which waited for: 0 -> 1; matrix products, arithmetic and copies ran while one was open for 28% -> 20% of each run, Pallas kernels for 0% -> 0%
where the time goes in v1:
time: 472 us; the launch traced here: 468 us
  waiting for transfers between devices  222 us (47%)
  starting transfers between devices  101 us (21%)
  matrix products  61.6 us (13%)
  other arithmetic  54.1 us (11%)
  between operations  15 us (3%)
  local copies, waits for them, and re-layouts  13 us (3%)
    all_gather x1, waiting for transfers between devices, local(): gram_matrix = jnp.sum(lax.all_gather(gram_local, ('blk', 'grp')), axis=0)  222 us
    ppermute x24, starting transfers between devices, passed_along(): return lax.ppermute(block, axis, route)  101 us
    dot_general x36, matrix products, tile_terms(): jnp.einsum('pe,cqe->cpq', row_points, col_points, preferred_element_type=...  51.9 us
    convert_element_type x36, other arithmetic, tile_terms(): row_scales.astype(jnp.float32)[None, :, None]  24.9 us
  transfers between devices with their start and end apart: 25, of which 1 were waited for; matrix products, arithmetic and copies ran while one was open for 20% of the time, Pallas kernels for 0%

profile of v1, /device:TPU:1, one launch (start us, length us, event | category | flops | bytes accessed | tf_op | source)
XLA Modules:
  0.0 468.3 jit_solution(8715827963982613735)
XLA Ops:
  8.2 4.4 collective-permute-start.2
  12.6 4.9 %collective-permute-start.5 = (bf16[64,4,256]{2,1,0:T(4,128)(2,1)S(1)}, bf16[64,4,256]{2,1,0:T(4,128)(2,1)S(1)}, u32[]{:S(2)}, u32[]{:S(2)}) collective-permute-start(bf16[64,4,256]{2,1,0:T(4,128)(2,1)S(1)} %reshape_squeeze.6), channel_id=1, source_target_pairs={{496,0},{504,8},{0,16},{8,24},{16,32},{24,40},{32,48},{40,56},{48,... | collective-permute-start | bytes 393224 | tf_op jit(solution)/shard_map/ppermute | solution.py:17
  17.5 7.5 %collective-permute-start.8 = (bf16[64,4,256]{2,1,0:T(4,128)(2,1)S(1)}, bf16[64,4,256]{2,1,0:T(4,128)(2,1)S(1)}, u32[]{:S(2)}, u32[]{:S(2)}) collective-permute-start(bf16[64,4,256]{2,1,0:T(4,128)(2,1)S(1)} %reshape_squeeze.6), channel_id=1, source_target_pairs={{488,0},{496,8},{504,16},{0,24},{8,32},{16,40},{24,48},{32,56},{40... | collective-permute-start | bytes 393224 | tf_op jit(solution)/shard_map/ppermute | solution.py:17
  25.0 7.0 %collective-permute-start.11 = (bf16[64,4,256]{2,1,0:T(4,128)(2,1)S(1)}, bf16[64,4,256]{2,1,0:T(4,128)(2,1)S(1)}, u32[]{:S(2)}, u32[]{:S(2)}) collective-permute-start(bf16[64,4,256]{2,1,0:T(4,128)(2,1)S(1)} %reshape_squeeze.6), channel_id=1, source_target_pairs={{480,0},{488,8},{496,16},{504,24},{0,32},{8,40},{16,48},{24,56},{3... | collective-permute-start | bytes 393224 | tf_op jit(solution)/shard_map/ppermute | solution.py:17
  32.0 2.6 collective-permute-start
  37.6 6.8 %gather_fusion = bf16[1024,128]{1,0:T(8,128)(2,1)S(1)} fusion(bf16[4,256,128]{2,1,0:T(8,128)(2,1)} %bitcast.507, s32[1024]{0:T(1024)S(1)} %bitcast.505), kind=kCustom, calls=%fused_computation | custom fusion | bytes 532480 | tf_op jit(solution)/shard_map/jit(take_along_axis)/gather | solution.py:46
  48.1 5.2 %collective-permute-start.14 = (bf16[64,4,256]{2,1,0:T(4,128)(2,1)S(1)}, bf16[64,4,256]{2,1,0:T(4,128)(2,1)S(1)}, u32[]{:S(2)}, u32[]{:S(2)}) collective-permute-start(bf16[64,4,256]{2,1,0:T(4,128)(2,1)S(1)} %reshape_squeeze.6), channel_id=1, source_target_pairs={{32,0},{40,8},{48,16},{56,24},{64,32},{72,40},{80,48},{88,56},{96,... | collective-permute-start | bytes 393224 | tf_op jit(solution)/shard_map/ppermute | solution.py:17
  53.3 3.6 collective-permute-start.17
  56.9 3.7 collective-permute-start.20
  60.6 3.1 collective-permute-start.23
  63.7 13.1 %while.109 = (s32[]{:T(128)}, f32[4,64,256]{2,1,0:T(8,128)S(1)}, f32[4,256]{1,0:T(4,128)S(1)}, f32[4,256]{1,0:T(4,128)S(1)}, bf16[4,256,128]{2,1,0:T(8,128)(2,1)...) while((s32[]{:T(128)}, f32[4,64,256]{2,1,0:T(8,128)S(1)}, ...), condition=%wide.region_5.6_spmd, body=%wide.region_3.0_spmd.sunk | while | flops 103023616 | bytes 1596585 | solution.py:77
  79.2 2.5 collective-permute-start.4
  81.8 5.2 %collective-permute-start.3 = (bf16[4,256,128]{2,1,0:T(8,128)(2,1)}, bf16[4,256,128]{2,1,0:T(8,128)(2,1)S(1)}, u32[]{:S(2)}, u32[]{:S(2)}) collective-permute-start(bf16[4,256,128]{2,1,0:T(8,128)(2,1)} %get-tuple-element.2157), channel_id=1, source_target_pairs={{496,0},{504,8},{0,16},{8,24},{16,32},{24,40},{32,48},{40,56},{48,... | collective-permute-start | bytes 786440 | tf_op jit(solution)/shard_map/ppermute | solution.py:17
  87.0 5.9 %collective-permute-start.7 = (bf16[4,256]{1,0:T(4,128)(2,1)}, bf16[4,256]{1,0:T(4,128)(2,1)S(1)}, u32[]{:S(2)}, u32[]{:S(2)}) collective-permute-start(bf16[4,256]{1,0:T(4,128)(2,1)} %convert_element_type.264), channel_id=1, source_target_pairs={{488,0},{496,8},{504,16},{0,24},{8,32},{16,40},{24,48},{32,56},{40... | collective-permute-start | bytes 6152 | tf_op jit(solution)/shard_map/ppermute | solution.py:17
  97.6 9.6 %while.110 = (s32[]{:T(128)}, f32[4,64,256]{2,1,0:T(8,128)S(1)}, f32[4,256]{1,0:T(4,128)S(1)}, f32[4,256]{1,0:T(4,128)S(1)}, f32[4,256]{1,0:T(4,128)S(1)}, /*ind...) while((s32[]{:T(128)}, f32[4,64,256]{2,1,0:T(8,128)S(1)}, ...), condition=%wide.region_10.11_spmd, body=%wide.region_8.10_spmd.sunk | while | flops 103023616 | bytes 1596609 | solution.py:77
  107.2 4.9 %collective-permute-start.9 = (bf16[4,256,128]{2,1,0:T(8,128)(2,1)}, bf16[4,256,128]{2,1,0:T(8,128)(2,1)S(1)}, u32[]{:S(2)}, u32[]{:S(2)}) collective-permute-start(bf16[4,256,128]{2,1,0:T(8,128)(2,1)} %get-tuple-element.2160), channel_id=1, source_target_pairs={{480,0},{488,8},{496,16},{504,24},{0,32},{8,40},{16,48},{24,56},{3... | collective-permute-start | bytes 786440 | tf_op jit(solution)/shard_map/ppermute | solution.py:17
  112.3 6.4 %collective-permute-start.13 = (bf16[4,256]{1,0:T(4,128)(2,1)}, bf16[4,256]{1,0:T(4,128)(2,1)S(1)}, u32[]{:S(2)}, u32[]{:S(2)}) collective-permute-start(bf16[4,256]{1,0:T(4,128)(2,1)} %convert_element_type.264), channel_id=1, source_target_pairs={{32,0},{40,8},{48,16},{56,24},{64,32},{72,40},{80,48},{88,56},{96,... | collective-permute-start | bytes 6152 | tf_op jit(solution)/shard_map/ppermute | solution.py:17
  118.8 9.6 %while.111 = (s32[]{:T(128)}, f32[4,64,256]{2,1,0:T(8,128)S(1)}, f32[4,256]{1,0:T(4,128)S(1)}, f32[4,256]{1,0:T(4,128)S(1)}, f32[4,256]{1,0:T(4,128)S(1)}, /*ind...) while((s32[]{:T(128)}, f32[4,64,256]{2,1,0:T(8,128)S(1)}, ...), condition=%wide.region_15.16_spmd, body=%wide.region_13.15_spmd.sunk | while | flops 103023616 | bytes 1596609 | solution.py:77
  128.4 7.3 %collective-permute-start.12 = (bf16[4,256,128]{2,1,0:T(8,128)(2,1)}, bf16[4,256,128]{2,1,0:T(8,128)(2,1)S(1)}, u32[]{:S(2)}, u32[]{:S(2)}) collective-permute-start(bf16[4,256,128]{2,1,0:T(8,128)(2,1)} %get-tuple-element.2162), channel_id=1, source_target_pairs={{32,0},{40,8},{48,16},{56,24},{64,32},{72,40},{80,48},{88,56},{96,... | collective-permute-start | bytes 786440 | tf_op jit(solution)/shard_map/ppermute | solution.py:17
  135.9 5.9 %collective-permute-start.16 = (bf16[4,256]{1,0:T(4,128)(2,1)}, bf16[4,256]{1,0:T(4,128)(2,1)S(1)}, u32[]{:S(2)}, u32[]{:S(2)}) collective-permute-start(bf16[4,256]{1,0:T(4,128)(2,1)} %convert_element_type.264), channel_id=1, source_target_pairs={{24,0},{32,8},{40,16},{48,24},{56,32},{64,40},{72,48},{80,56},{88,... | collective-permute-start | bytes 6152 | tf_op jit(solution)/shard_map/ppermute | solution.py:17
  141.9 9.6 %while.112 = (s32[]{:T(128)}, f32[4,64,256]{2,1,0:T(8,128)S(1)}, f32[4,256]{1,0:T(4,128)S(1)}, f32[4,256]{1,0:T(4,128)S(1)}, f32[4,256]{1,0:T(4,128)S(1)}, /*ind...) while((s32[]{:T(128)}, f32[4,64,256]{2,1,0:T(8,128)S(1)}, ...), condition=%wide.region_20.21_spmd, body=%wide.region_18.20_spmd.sunk | while | flops 103023616 | bytes 1596609 | solution.py:77
  156.1 9.6 %while.113 = (s32[]{:T(128)}, f32[4,64,256]{2,1,0:T(8,128)S(1)}, f32[4,256]{1,0:T(4,128)S(1)}, f32[4,256]{1,0:T(4,128)S(1)}, f32[4,256]{1,0:T(4,128)S(1)}, /*ind...) while((s32[]{:T(128)}, f32[4,64,256]{2,1,0:T(8,128)S(1)}, ...), condition=%wide.region_25.26_spmd, body=%wide.region_23.25_spmd.sunk | while | flops 103023616 | bytes 1596609 | solution.py:77
  165.8 4.8 %collective-permute-start.18 = (bf16[4,256,128]{2,1,0:T(8,128)(2,1)}, bf16[4,256,128]{2,1,0:T(8,128)(2,1)S(1)}, u32[]{:S(2)}, u32[]{:S(2)}) collective-permute-start(bf16[4,256,128]{2,1,0:T(8,128)(2,1)} %get-tuple-element.2166), channel_id=1, source_target_pairs={{16,0},{24,8},{32,16},{40,24},{48,32},{56,40},{64,48},{72,56},{80,... | collective-permute-start | bytes 786440 | tf_op jit(solution)/shard_map/ppermute | solution.py:17
  170.8 3.1 collective-permute-start.22
  174.0 9.6 %while.114 = (s32[]{:T(128)}, f32[4,64,256]{2,1,0:T(8,128)S(1)}, f32[4,256]{1,0:T(4,128)S(1)}, f32[4,256]{1,0:T(4,128)S(1)}, f32[4,256]{1,0:T(4,128)S(1)}, /*ind...) while((s32[]{:T(128)}, f32[4,64,256]{2,1,0:T(8,128)S(1)}, ...), condition=%wide.region_30.31_spmd, body=%wide.region_28.30_spmd.sunk | while | flops 103023616 | bytes 1596609 | solution.py:77
  186.0 9.6 %while.115 = (s32[]{:T(128)}, f32[4,64,256]{2,1,0:T(8,128)S(1)}, f32[4,256]{1,0:T(4,128)S(1)}, f32[4,256]{1,0:T(4,128)S(1)}, f32[4,256]{1,0:T(4,128)S(1)}, /*ind...) while((s32[]{:T(128)}, f32[4,64,256]{2,1,0:T(8,128)S(1)}, ...), condition=%wide.region_35.36_spmd, body=%wide.region_33.35_spmd.sunk | while | flops 103023616 | bytes 1596609 | solution.py:77
  195.9 9.6 %while.116 = (s32[]{:T(128)}, f32[4,64,256]{2,1,0:T(8,128)S(1)}, f32[4,256]{1,0:T(4,128)S(1)}, f32[4,256]{1,0:T(4,128)S(1)}, f32[4,256]{1,0:T(4,128)S(1)}, /*ind...) while((s32[]{:T(128)}, f32[4,64,256]{2,1,0:T(8,128)S(1)}, ...), condition=%wide.region_40.41_spmd, body=%wide.region_38.40_spmd.sunk | while | flops 103023616 | bytes 1596609 | solution.py:77
  206.8 10.2 %while.117 = (s32[]{:T(128)}, f32[4,64,256]{2,1,0:T(8,128)S(1)}, f32[4,256]{1,0:T(4,128)S(1)}, f32[4,256]{1,0:T(4,128)S(1)}, f32[4,256]{1,0:T(4,128)S(1)}, /*ind...) while((s32[]{:T(128)}, f32[4,64,256]{2,1,0:T(8,128)S(1)}, ...), condition=%wide.region_45.46_spmd, body=%wide.region_43.45_spmd.sunk | while | flops 103023616 | bytes 1596609 | solution.py:77
  218.2 222.3 %all-gather.3.cloned.1.call-done = f32[32768,64]{1,0:T(8,128)} async-done(((f32[64,64]{1,0:T(8,128)}), f32[32768,64]{1,0:T(8,128)}) %all-gather.3.cloned.1.call-update) | async-done | bytes 8388624 | tf_op jit(solution)/shard_map/all_gather | solution.py:96
  440.5 6.9 %reduce_sum.198 = f32[64,64]{1,0:T(8,128)S(1)} reduce(f32[512,64,64]{2,1,0:T(8,128)} %bitcast.509, f32[]{:T(128)} %constant.264.clone.1), dimensions={0}, to_apply=%region_46.47 | reduce | flops 2093056 | bytes 8404996 | tf_op jit(solution)/shard_map/reduce_sum | solution.py:96
  447.5 5.8 %cholesky.16 = f32[64,64]{1,0:T(8,128)S(1)} custom-call(f32[64,64]{1,0:T(8,128)S(1)} %fusion.123), custom_call_target="Cholesky" | custom-call | tf_op jit(solution)/shard_map/jit(cholesky)/cholesky | solution.py:97
  454.7 4.9 %custom-call.6 = f32[1,64,64]{1,2,0:T(8,128)S(1)} custom-call(f32[1,64,64]{2,1,0:T(8,128)S(1)} %get-tuple-element.1165), custom_call_target="InvertDiagBlocksLowerTriangular" | custom-call | tf_op jit(solution)/shard_map/triangular_solve | solution.py:98
  (362 shorter events, 117.2 us)
Async XLA Ops:
  7.2 27.6 %copy-start = (s32[1,256,16]{1,2,0:T(8,128)S(1)}, s32[1,256,16]{1,2,0:T(8,128)}, u32[]{:S(2)}) copy-start(s32[1,256,16]{1,2,0:T(8,128)} %param.26) | copy-start | bytes 49156
  7.2 433.3 %all-gather.3.cloned.1.call-start = ((), (), s32[]{:S(2)}) async-start(), calls=%async_computation | async-start | bytes 16809984 | tf_op jit(solution)/shard_map/all_gather | solution.py:96
  8.2 39.9 %collective-permute-start.2 = (bf16[64,4,256]{2,1,0:T(4,128)(2,1)S(1)}, bf16[64,4,256]{2,1,0:T(4,128)(2,1)S(1)}, u32[]{:S(2)}, u32[]{:S(2)}) collective-permute-start(bf16[64,4,256]{2,1,0:T(4,128)(2,1)S(1)} %reshape_squeeze.6), channel_id=1, source_target_pairs={{504,0},{0,8},{8,16},{16,24},{24,32},{32,40},{40,48},{48,56},{56,6... | collective-permute-start | bytes 393224 | tf_op jit(solution)/shard_map/ppermute | solution.py:17
  12.6 40.7 %collective-permute-start.5 = (bf16[64,4,256]{2,1,0:T(4,128)(2,1)S(1)}, bf16[64,4,256]{2,1,0:T(4,128)(2,1)S(1)}, u32[]{:S(2)}, u32[]{:S(2)}) collective-permute-start(bf16[64,4,256]{2,1,0:T(4,128)(2,1)S(1)} %reshape_squeeze.6), channel_id=1, source_target_pairs={{496,0},{504,8},{0,16},{8,24},{16,32},{24,40},{32,48},{40,56},{48,... | collective-permute-start | bytes 393224 | tf_op jit(solution)/shard_map/ppermute | solution.py:17
  17.5 39.4 %collective-permute-start.8 = (bf16[64,4,256]{2,1,0:T(4,128)(2,1)S(1)}, bf16[64,4,256]{2,1,0:T(4,128)(2,1)S(1)}, u32[]{:S(2)}, u32[]{:S(2)}) collective-permute-start(bf16[64,4,256]{2,1,0:T(4,128)(2,1)S(1)} %reshape_squeeze.6), channel_id=1, source_target_pairs={{488,0},{496,8},{504,16},{0,24},{8,32},{16,40},{24,48},{32,56},{40... | collective-permute-start | bytes 393224 | tf_op jit(solution)/shard_map/ppermute | solution.py:17
  25.0 35.6 %collective-permute-start.11 = (bf16[64,4,256]{2,1,0:T(4,128)(2,1)S(1)}, bf16[64,4,256]{2,1,0:T(4,128)(2,1)S(1)}, u32[]{:S(2)}, u32[]{:S(2)}) collective-permute-start(bf16[64,4,256]{2,1,0:T(4,128)(2,1)S(1)} %reshape_squeeze.6), channel_id=1, source_target_pairs={{480,0},{488,8},{496,16},{504,24},{0,32},{8,40},{16,48},{24,56},{3... | collective-permute-start | bytes 393224 | tf_op jit(solution)/shard_map/ppermute | solution.py:17
  32.0 61.0 %collective-permute-start = (bf16[4,256,128]{2,1,0:T(8,128)(2,1)}, bf16[4,256,128]{2,1,0:T(8,128)(2,1)S(1)}, u32[]{:S(2)}, u32[]{:S(2)}) collective-permute-start(bf16[4,256,128]{2,1,0:T(8,128)(2,1)} %bitcast.506), channel_id=1, source_target_pairs={{504,0},{0,8},{8,16},{16,24},{24,32},{32,40},{40,48},{48,56},{56,6... | collective-permute-start | bytes 786440 | tf_op jit(solution)/shard_map/ppermute | solution.py:17
  48.1 28.9 %collective-permute-start.14 = (bf16[64,4,256]{2,1,0:T(4,128)(2,1)S(1)}, bf16[64,4,256]{2,1,0:T(4,128)(2,1)S(1)}, u32[]{:S(2)}, u32[]{:S(2)}) collective-permute-start(bf16[64,4,256]{2,1,0:T(4,128)(2,1)S(1)} %reshape_squeeze.6), channel_id=1, source_target_pairs={{32,0},{40,8},{48,16},{56,24},{64,32},{72,40},{80,48},{88,56},{96,... | collective-permute-start | bytes 393224 | tf_op jit(solution)/shard_map/ppermute | solution.py:17
  53.3 25.9 %collective-permute-start.17 = (bf16[64,4,256]{2,1,0:T(4,128)(2,1)S(1)}, bf16[64,4,256]{2,1,0:T(4,128)(2,1)S(1)}, u32[]{:S(2)}, u32[]{:S(2)}) collective-permute-start(bf16[64,4,256]{2,1,0:T(4,128)(2,1)S(1)} %reshape_squeeze.6), channel_id=1, source_target_pairs={{24,0},{32,8},{40,16},{48,24},{56,32},{64,40},{72,48},{80,56},{88,... | collective-permute-start | bytes 393224 | tf_op jit(solution)/shard_map/ppermute | solution.py:17
  56.9 24.9 %collective-permute-start.20 = (bf16[64,4,256]{2,1,0:T(4,128)(2,1)S(1)}, bf16[64,4,256]{2,1,0:T(4,128)(2,1)S(1)}, u32[]{:S(2)}, u32[]{:S(2)}) collective-permute-start(bf16[64,4,256]{2,1,0:T(4,128)(2,1)S(1)} %reshape_squeeze.6), channel_id=1, source_target_pairs={{16,0},{24,8},{32,16},{40,24},{48,32},{56,40},{64,48},{72,56},{80,... | collective-permute-start | bytes 393224 | tf_op jit(solution)/shard_map/ppermute | solution.py:17
  60.6 26.5 %collective-permute-start.23 = (bf16[64,4,256]{2,1,0:T(4,128)(2,1)S(1)}, bf16[64,4,256]{2,1,0:T(4,128)(2,1)S(1)}, u32[]{:S(2)}, u32[]{:S(2)}) collective-permute-start(bf16[64,4,256]{2,1,0:T(4,128)(2,1)S(1)} %reshape_squeeze.6), channel_id=1, source_target_pairs={{8,0},{16,8},{24,16},{32,24},{40,32},{48,40},{56,48},{64,56},{72,6... | collective-permute-start | bytes 393224 | tf_op jit(solution)/shard_map/ppermute | solution.py:17
  77.0 18.6 %collective-permute-start.1 = (bf16[4,256]{1,0:T(4,128)(2,1)}, bf16[4,256]{1,0:T(4,128)(2,1)S(1)}, u32[]{:S(2)}, u32[]{:S(2)}) collective-permute-start(bf16[4,256]{1,0:T(4,128)(2,1)} %convert_element_type.264), channel_id=1, source_target_pairs={{504,0},{0,8},{8,16},{16,24},{24,32},{32,40},{40,48},{48,56},{56,6... | collective-permute-start | bytes 6152 | tf_op jit(solution)/shard_map/ppermute | solution.py:17
  79.2 33.1 %collective-permute-start.4 = (bf16[4,256]{1,0:T(4,128)(2,1)}, bf16[4,256]{1,0:T(4,128)(2,1)S(1)}, u32[]{:S(2)}, u32[]{:S(2)}) collective-permute-start(bf16[4,256]{1,0:T(4,128)(2,1)} %convert_element_type.264), channel_id=1, source_target_pairs={{496,0},{504,8},{0,16},{8,24},{16,32},{24,40},{32,48},{40,56},{48,... | collective-permute-start | bytes 6152 | tf_op jit(solution)/shard_map/ppermute | solution.py:17
  81.8 25.4 %collective-permute-start.3 = (bf16[4,256,128]{2,1,0:T(8,128)(2,1)}, bf16[4,256,128]{2,1,0:T(8,128)(2,1)S(1)}, u32[]{:S(2)}, u32[]{:S(2)}) collective-permute-start(bf16[4,256,128]{2,1,0:T(8,128)(2,1)} %get-tuple-element.2157), channel_id=1, source_target_pairs={{496,0},{504,8},{0,16},{8,24},{16,32},{24,40},{32,48},{40,56},{48,... | collective-permute-start | bytes 786440 | tf_op jit(solution)/shard_map/ppermute | solution.py:17
  87.0 48.9 %collective-permute-start.7 = (bf16[4,256]{1,0:T(4,128)(2,1)}, bf16[4,256]{1,0:T(4,128)(2,1)S(1)}, u32[]{:S(2)}, u32[]{:S(2)}) collective-permute-start(bf16[4,256]{1,0:T(4,128)(2,1)} %convert_element_type.264), channel_id=1, source_target_pairs={{488,0},{496,8},{504,16},{0,24},{8,32},{16,40},{24,48},{32,56},{40... | collective-permute-start | bytes 6152 | tf_op jit(solution)/shard_map/ppermute | solution.py:17
  93.0 35.5 %collective-permute-start.6 = (bf16[4,256,128]{2,1,0:T(8,128)(2,1)}, bf16[4,256,128]{2,1,0:T(8,128)(2,1)S(1)}, u32[]{:S(2)}, u32[]{:S(2)}) collective-permute-start(bf16[4,256,128]{2,1,0:T(8,128)(2,1)} %get-tuple-element.2157), channel_id=1, source_target_pairs={{488,0},{496,8},{504,16},{0,24},{8,32},{16,40},{24,48},{32,56},{40... | collective-permute-start | bytes 786440 | tf_op jit(solution)/shard_map/ppermute | solution.py:17
  95.6 58.6 %collective-permute-start.10 = (bf16[4,256]{1,0:T(4,128)(2,1)}, bf16[4,256]{1,0:T(4,128)(2,1)S(1)}, u32[]{:S(2)}, u32[]{:S(2)}) collective-permute-start(bf16[4,256]{1,0:T(4,128)(2,1)} %convert_element_type.264), channel_id=1, source_target_pairs={{480,0},{488,8},{496,16},{504,24},{0,32},{8,40},{16,48},{24,56},{3... | collective-permute-start | bytes 6152 | tf_op jit(solution)/shard_map/ppermute | solution.py:17
  107.2 44.3 %collective-permute-start.9 = (bf16[4,256,128]{2,1,0:T(8,128)(2,1)}, bf16[4,256,128]{2,1,0:T(8,128)(2,1)S(1)}, u32[]{:S(2)}, u32[]{:S(2)}) collective-permute-start(bf16[4,256,128]{2,1,0:T(8,128)(2,1)} %get-tuple-element.2160), channel_id=1, source_target_pairs={{480,0},{488,8},{496,16},{504,24},{0,32},{8,40},{16,48},{24,56},{3... | collective-permute-start | bytes 786440 | tf_op jit(solution)/shard_map/ppermute | solution.py:17
  112.3 58.5 %collective-permute-start.13 = (bf16[4,256]{1,0:T(4,128)(2,1)}, bf16[4,256]{1,0:T(4,128)(2,1)S(1)}, u32[]{:S(2)}, u32[]{:S(2)}) collective-permute-start(bf16[4,256]{1,0:T(4,128)(2,1)} %convert_element_type.264), channel_id=1, source_target_pairs={{32,0},{40,8},{48,16},{56,24},{64,32},{72,40},{80,48},{88,56},{96,... | collective-permute-start | bytes 6152 | tf_op jit(solution)/shard_map/ppermute | solution.py:17
  128.4 37.3 %collective-permute-start.12 = (bf16[4,256,128]{2,1,0:T(8,128)(2,1)}, bf16[4,256,128]{2,1,0:T(8,128)(2,1)S(1)}, u32[]{:S(2)}, u32[]{:S(2)}) collective-permute-start(bf16[4,256,128]{2,1,0:T(8,128)(2,1)} %get-tuple-element.2162), channel_id=1, source_target_pairs={{32,0},{40,8},{48,16},{56,24},{64,32},{72,40},{80,48},{88,56},{96,... | collective-permute-start | bytes 786440 | tf_op jit(solution)/shard_map/ppermute | solution.py:17
  135.9 50.0 %collective-permute-start.16 = (bf16[4,256]{1,0:T(4,128)(2,1)}, bf16[4,256]{1,0:T(4,128)(2,1)S(1)}, u32[]{:S(2)}, u32[]{:S(2)}) collective-permute-start(bf16[4,256]{1,0:T(4,128)(2,1)} %convert_element_type.264), channel_id=1, source_target_pairs={{24,0},{32,8},{40,16},{48,24},{56,32},{64,40},{72,48},{80,56},{88,... | collective-permute-start | bytes 6152 | tf_op jit(solution)/shard_map/ppermute | solution.py:17
  151.5 32.1 %collective-permute-start.15 = (bf16[4,256,128]{2,1,0:T(8,128)(2,1)}, bf16[4,256,128]{2,1,0:T(8,128)(2,1)S(1)}, u32[]{:S(2)}, u32[]{:S(2)}) collective-permute-start(bf16[4,256,128]{2,1,0:T(8,128)(2,1)} %get-tuple-element.2164), channel_id=1, source_target_pairs={{24,0},{32,8},{40,16},{48,24},{56,32},{64,40},{72,48},{80,56},{88,... | collective-permute-start | bytes 786440 | tf_op jit(solution)/shard_map/ppermute | solution.py:17
  154.2 41.7 %collective-permute-start.19 = (bf16[4,256]{1,0:T(4,128)(2,1)}, bf16[4,256]{1,0:T(4,128)(2,1)S(1)}, u32[]{:S(2)}, u32[]{:S(2)}) collective-permute-start(bf16[4,256]{1,0:T(4,128)(2,1)} %convert_element_type.264), channel_id=1, source_target_pairs={{16,0},{24,8},{32,16},{40,24},{48,32},{56,40},{64,48},{72,56},{80,... | collective-permute-start | bytes 6152 | tf_op jit(solution)/shard_map/ppermute | solution.py:17
  165.8 29.8 %collective-permute-start.18 = (bf16[4,256,128]{2,1,0:T(8,128)(2,1)}, bf16[4,256,128]{2,1,0:T(8,128)(2,1)S(1)}, u32[]{:S(2)}, u32[]{:S(2)}) collective-permute-start(bf16[4,256,128]{2,1,0:T(8,128)(2,1)} %get-tuple-element.2166), channel_id=1, source_target_pairs={{16,0},{24,8},{32,16},{40,24},{48,32},{56,40},{64,48},{72,56},{80,... | collective-permute-start | bytes 786440 | tf_op jit(solution)/shard_map/ppermute | solution.py:17
  170.8 35.9 %collective-permute-start.22 = (bf16[4,256]{1,0:T(4,128)(2,1)}, bf16[4,256]{1,0:T(4,128)(2,1)S(1)}, u32[]{:S(2)}, u32[]{:S(2)}) collective-permute-start(bf16[4,256]{1,0:T(4,128)(2,1)} %convert_element_type.264), channel_id=1, source_target_pairs={{8,0},{16,8},{24,16},{32,24},{40,32},{48,40},{56,48},{64,56},{72,6... | collective-permute-start | bytes 6152 | tf_op jit(solution)/shard_map/ppermute | solution.py:17
  183.6 21.9 %collective-permute-start.21 = (bf16[4,256,128]{2,1,0:T(8,128)(2,1)}, bf16[4,256,128]{2,1,0:T(8,128)(2,1)}, u32[]{:S(2)}, u32[]{:S(2)}) collective-permute-start(bf16[4,256,128]{2,1,0:T(8,128)(2,1)} %get-tuple-element.2168), channel_id=1, source_target_pairs={{8,0},{16,8},{24,16},{32,24},{40,32},{48,40},{56,48},{64,56},{72,6... | collective-permute-start | bytes 786440 | tf_op jit(solution)/shard_map/ppermute | solution.py:17
Sparse Core Ops, SparseCore 0:
  218.3 222.1 all-gather.2
